TPU v7x, 256 devices: a whole 4x4x8 slice. The times are simulated.
256 devices in a mesh: cell: 64 (over y, z, core), view: 4 (over x).
Axes of the slice: x: 4, y: 4, z: 8, core: 2. Of those that a mesh axis runs over, the one named last changes fastest.
Arguments:
- gaussians: float32 [1024, 9, 256], P('cell'), as said below
- seg_count: int32 [4, 64], P('view', 'cell'), may hold values from 1 to 3, as said below
- seg_block: int32 [4, 64, 3], P('view', 'cell'), may hold values from 0 to 1023, as said below
- ray_count: int32 [4, 64], P('view', 'cell'), may hold values from 576 to 2304
- camera_shift: float32 [4, 2], P('view'), may hold values from -6 to 6
- target: float32 [4, 64, 3, 2304], P('view', 'cell'), may hold values from 0 to 1
Outputs:
- image: float32 [4, 64, 3, 2304], P('view', 'cell')
- gauss_grad: float32 [1024, 9, 256], P('cell')
Inputs may be any that keep to these rules, and one draw needn't show every extreme that they name: `gaussians`: each column of a block is one Gaussian: a mean, the entries a, b, c of a positive definite inverse covariance, an opacity in (0, 1), three colours. `seg_count`: tiles 2m and 2m + 1 of a view hold 4 segments together; in every view some tile holds 3. Segment k of tile t uses a block stored in cell seg_block // 16, which is t + e modulo 64 for some e from -2 to 2; entries at k >= seg_count are not used.
All inputs are finite; a program needn't handle non-finite values.
Results may differ from a plain program's by a relative error of at most 0.0003.
Values sent between devices are 32-bit elements; how exact they have to be, the bound alone decides.
No kernel may reach another device: no remote copies, remote signals or barrier semaphores. Data moves between devices by JAX's collectives and lax.ppermute only.
A program may use at most 64 MiB of HBM per device.

v0:
```python
import jax
import jax.numpy as jnp
from jax import lax
from jax.sharding import PartitionSpec as P

TILE = 48
REACH = 2
precise = lax.Precision.HIGHEST


def shifted(block, axis, distance):
    devices = range(lax.axis_size(axis))
    route = [((i - distance) % len(devices), i) for i in devices]
    return lax.ppermute(block, axis, route)


def pixel_frame(shift, pixels):
    pixel_ids = jnp.arange(pixels)
    centre = (TILE - 1) / 2.0
    pix_x = (pixel_ids % TILE).astype(jnp.float32) - centre - shift[0]
    pix_y = (pixel_ids // TILE).astype(jnp.float32) - centre - shift[1]
    return (pix_x, pix_y)


def triangles(length):
    row_ids = lax.broadcasted_iota(jnp.int32, (length, length), 0)
    col_ids = lax.broadcasted_iota(jnp.int32, (length, length), 1)
    return ((col_ids < row_ids).astype(jnp.float32), (col_ids > row_ids).astype(jnp.float32))


def splat(params, pix_x, pix_y):
    delta_x = pix_x[None, :] - params[0][:, None]
    delta_y = pix_y[None, :] - params[1][:, None]
    quad_form = (
        params[2][:, None] * delta_x * delta_x
        + 2.0 * params[3][:, None] * delta_x * delta_y
        + params[4][:, None] * delta_y * delta_y
    )
    alphas = params[5][:, None] * jnp.exp(-0.5 * quad_form)
    return (alphas, jnp.log1p(-alphas))


def forward_task(params, pix_x, pix_y, lower_tri):
    alphas, log_trans = splat(params, pix_x, pix_y)
    prefix = jnp.dot(lower_tri, log_trans, precision=precise, preferred_element_type=jnp.float32)
    weights = alphas * jnp.exp(prefix)
    colour = jnp.dot(params[6:9], weights, precision=precise, preferred_element_type=jnp.float32)
    totals = jnp.sum(log_trans, axis=0)
    return jnp.concatenate([colour, totals[None, :]], axis=0)


def gradient_rows(params, pix_x, pix_y, weighted, weights, weight_cot):
    features = jnp.stack(
        [jnp.ones_like(pix_x), pix_x, pix_y, pix_x * pix_x, pix_x * pix_y, pix_y * pix_y]
    )
    moments = lax.dot_general(
        features,
        weighted,
        (((1,), (1,)), ((), ())),
        precision=precise,
        preferred_element_type=jnp.float32,
    )
    colour_grad = lax.dot_general(
        weight_cot,
        weights,
        (((1,), (1,)), ((), ())),
        precision=precise,
        preferred_element_type=jnp.float32,
    )
    mean_x, mean_y, conic_a, conic_b, conic_c, opacity = (
        params[0],
        params[1],
        params[2],
        params[3],
        params[4],
        params[5],
    )
    moment_zero = moments[0]
    along_x = moments[1] - mean_x * moment_zero
    along_y = moments[2] - mean_y * moment_zero
    square_x = moments[3] - 2.0 * mean_x * moments[1] + mean_x * mean_x * moment_zero
    cross_xy = (
        moments[4] - mean_x * moments[2] - mean_y * moments[1] + mean_x * mean_y * moment_zero
    )
    square_y = moments[5] - 2.0 * mean_y * moments[2] + mean_y * mean_y * moment_zero
    grad_rows = jnp.stack(
        [
            conic_a * along_x + conic_b * along_y,
            conic_b * along_x + conic_c * along_y,
            -0.5 * square_x,
            -cross_xy,
            -0.5 * square_y,
            moment_zero / opacity,
        ]
    )
    return jnp.concatenate([grad_rows, colour_grad], axis=0)


def backward_task(params, cotangent, pix_x, pix_y, lower_tri, upper_tri):
    alphas, log_trans = splat(params, pix_x, pix_y)
    transmit = jnp.exp(
        jnp.dot(lower_tri, log_trans, precision=precise, preferred_element_type=jnp.float32)
    )
    weights = alphas * transmit
    weight_cot = cotangent[:3]
    shaded = lax.dot_general(
        params[6:9],
        weight_cot,
        (((0,), (0,)), ((), ())),
        precision=precise,
        preferred_element_type=jnp.float32,
    )
    later_sum = jnp.dot(
        upper_tri, weights * shaded, precision=precise, preferred_element_type=jnp.float32
    )
    dalpha = transmit * shaded - (later_sum + cotangent[3][None, :]) / (1.0 - alphas)
    return gradient_rows(params, pix_x, pix_y, dalpha * alphas, weights, weight_cot)


def composite(partials, live_mask, target_tile, valid_slot):
    slot_total = partials.shape[0]
    running = jnp.zeros(partials.shape[2:], jnp.float32)
    transmit = []
    for slot_index in range(slot_total):
        transmit.append(jnp.exp(running))
        running = running + partials[slot_index, 3]
    transmit = jnp.stack(transmit)
    shaded = transmit[:, None, :] * partials[:, :3]
    rendered = jnp.sum(shaded, axis=0) * live_mask
    residual = (rendered - target_tile) * live_mask
    behind = []
    running_sum = jnp.zeros_like(rendered)
    for slot_index in range(slot_total - 1, -1, -1):
        behind.insert(0, running_sum)
        running_sum = running_sum + shaded[slot_index]
    behind = jnp.stack(behind)
    valid_weight = valid_slot.astype(jnp.float32)
    weight_cot = transmit[:, None, :] * residual[None] * valid_weight[:, None, None]
    after_cot = jnp.sum(residual[None] * behind, axis=1) * valid_weight[:, None]
    return (rendered, jnp.concatenate([weight_cot, after_cot[:, None, :]], axis=1))


def shards(gaussians, seg_count, seg_block, ray_count, camera_shift, target):
    cell_count = lax.axis_size("cell")
    cell_index = lax.axis_index("cell")
    per_block = gaussians.shape[0]
    pixels = target.shape[3]
    lower_tri, upper_tri = triangles(gaussians.shape[2])
    blocks = seg_block[0, 0]
    slot_count = blocks.shape[0]
    own_count = seg_count[0, 0]
    home_cell = blocks // per_block
    local_block = blocks % per_block
    offset = (home_cell - cell_index + REACH) % cell_count - REACH
    pix_x, pix_y = pixel_frame(camera_shift[0], pixels)
    valid_slot = jnp.arange(slot_count) < own_count

    def run_forward(params):
        return forward_task(params, pix_x, pix_y, lower_tri)

    def run_backward(bundle):
        return backward_task(bundle[0], bundle[1], pix_x, pix_y, lower_tri, upper_tri)

    near_list = []
    for shift_by in range(-REACH, REACH + 1):
        if shift_by == 0:
            near_list.append(gaussians)
        else:
            near_list.append(shifted(gaussians, "cell", -shift_by))
    near_stack = jnp.concatenate(near_list, axis=0)
    pick_index = (offset + REACH) * per_block + local_block
    own_params = jnp.take(near_stack, pick_index, axis=0)
    partials = lax.map(run_forward, own_params)
    partials = jnp.where(valid_slot[:, None, None], partials, 0.0)
    live_mask = (jnp.arange(pixels) < ray_count[0, 0]).astype(jnp.float32)
    rendered, cotangent = composite(partials, live_mask, target[0, 0], valid_slot)
    own_grads = lax.map(run_backward, (own_params, cotangent))
    spot_count = (2 * REACH + 1) * per_block
    onehot = (pick_index[:, None] == jnp.arange(spot_count)[None, :]).astype(jnp.float32)
    spread = jnp.einsum("sk,sjg->kjg", onehot, own_grads, precision=precise)
    spread = spread.reshape((2 * REACH + 1, per_block) + gaussians.shape[1:])
    block_grads = spread[REACH]
    for shift_by in range(-REACH, REACH + 1):
        if shift_by != 0:
            block_grads = block_grads + shifted(spread[shift_by + REACH], "cell", shift_by)
    gauss_grad = lax.psum(block_grads, "view")
    return (rendered[None, None], gauss_grad)


def solution(mesh):
    placed = (
        P("cell", None, None),
        P("view", "cell"),
        P("view", "cell", None),
        P("view", "cell"),
        P("view", None),
        P("view", "cell", None, None),
    )
    return jax.shard_map(
        shards,
        mesh=mesh,
        in_specs=placed,
        out_specs=(P("view", "cell", None, None), P("cell", None, None)),
        check_vma=False,
    )
```

profile of v0, /device:TPU:8, one launch (start us, length us, event | category | flops | bytes accessed | tf_op | source)
XLA Modules:
  0.0 183.9 jit_solution(16609155894614825310)
XLA Ops:
  10.2 3.9 %collective-permute-start.2 = (f32[16,9,256]{2,1,0:T(8,128)S(1)}, f32[16,9,256]{2,1,0:T(8,128)S(1)}, u32[]{:S(2)}, u32[]{:S(2)}) collective-permute-start(f32[16,9,256]{2,1,0:T(8,128)S(1)} %copy.22), channel_id=1, source_target_pairs={{4,0},{8,4},{12,8},{16,12},{20,16},{24,20},{28,24},{32,28},{36,32}... | collective-permute-start | bytes 442376 | tf_op jit(solution)/shard_map/ppermute | solution.py:14
  29.0 30.8 %while.26 = (s32[]{:T(128)}, f32[3,4,2304]{2,1,0:T(4,128)S(1)}, f32[3,9,256]{2,1,0:T(8,128)S(1)}, f32[]{:T(128)}, f32[]{:T(128)}) while((s32[]{:T(128)}, f32[3,4,2304]{2,1,0:T(4,128)S(1)}, f32[3,9,256]{2,1,0:T(8,128)S(1)}, f32[]{:T(128)}, f32[]{:T(128)}) %tuple.102), condition=%wide.region_2.3_spmd.clone.clone, body=%wide.region_0.2_spmd.clone.sunk.clone | while | flops 1856945664 | bytes 4940977 | solution.py:173
  30.2 4.6 %fusion.187 = f32[256,2304]{0,1:T(8,128)S(1)} fusion(f32[256]{0:T(256)S(1)} %bitcast.284, f32[256]{0:T(256)S(1)} %bitcast.276, f32[2304]{0:T(1024)S(1)} %get-tuple-element.382, f32[256]{0:T(256)S(1)} %bitcast.278, f32[256]{0:T(256)S(1)} %bitcast.280, f32[2304]{0:T(1024)S(1)} %get-tuple-element.385, f32[256]{0:T(256)S(1)} %bitcast.282, ...), kind=kOutput, calls=%fused_computation.19.clone.1.clone | convolution fusion | flops 1827405824 | bytes 2383872 | tf_op jit(solution)/shard_map/while/body/eval_jaxpr/dot_general | solution.py:45
  36.9 2.3 %fusion.186 = f32[2304]{0:T(1024)S(1)} fusion(f32[256]{0:T(256)S(1)} %bitcast.285, f32[256]{0:T(256)S(1)} %bitcast.277, f32[2304]{0:T(1024)S(1)} %get-tuple-element.382, f32[256]{0:T(256)S(1)} %bitcast.279, f32[256]{0:T(256)S(1)} %bitcast.281, f32[2304]{0:T(1024)S(1)} %get-tuple-element.385, f32[256]{0:T(256)S(1)} %bitcast.283, f32[256]{0:T(256)S(1)} %bitcast.275), kind=kLoop, calls=%fused_computation.26.clone.1.clone | loop fusion | flops 8255232 | bytes 33792 | tf_op jit(solution)/shard_map/while/body/eval_jaxpr/reduce_sum | solution.py:48
  40.5 4.6 %fusion.187 = f32[256,2304]{0,1:T(8,128)S(1)} fusion(f32[256]{0:T(256)S(1)} %bitcast.284, f32[256]{0:T(256)S(1)} %bitcast.276, f32[2304]{0:T(1024)S(1)} %get-tuple-element.382, f32[256]{0:T(256)S(1)} %bitcast.278, f32[256]{0:T(256)S(1)} %bitcast.280, f32[2304]{0:T(1024)S(1)} %get-tuple-element.385, f32[256]{0:T(256)S(1)} %bitcast.282, ...), kind=kOutput, calls=%fused_computation.19.clone.1.clone | convolution fusion | flops 1827405824 | bytes 2383872 | tf_op jit(solution)/shard_map/while/body/eval_jaxpr/dot_general | solution.py:45
  47.1 2.3 %fusion.186 = f32[2304]{0:T(1024)S(1)} fusion(f32[256]{0:T(256)S(1)} %bitcast.285, f32[256]{0:T(256)S(1)} %bitcast.277, f32[2304]{0:T(1024)S(1)} %get-tuple-element.382, f32[256]{0:T(256)S(1)} %bitcast.279, f32[256]{0:T(256)S(1)} %bitcast.281, f32[2304]{0:T(1024)S(1)} %get-tuple-element.385, f32[256]{0:T(256)S(1)} %bitcast.283, f32[256]{0:T(256)S(1)} %bitcast.275), kind=kLoop, calls=%fused_computation.26.clone.1.clone | loop fusion | flops 8255232 | bytes 33792 | tf_op jit(solution)/shard_map/while/body/eval_jaxpr/reduce_sum | solution.py:48
  50.8 4.6 %fusion.187 = f32[256,2304]{0,1:T(8,128)S(1)} fusion(f32[256]{0:T(256)S(1)} %bitcast.284, f32[256]{0:T(256)S(1)} %bitcast.276, f32[2304]{0:T(1024)S(1)} %get-tuple-element.382, f32[256]{0:T(256)S(1)} %bitcast.278, f32[256]{0:T(256)S(1)} %bitcast.280, f32[2304]{0:T(1024)S(1)} %get-tuple-element.385, f32[256]{0:T(256)S(1)} %bitcast.282, ...), kind=kOutput, calls=%fused_computation.19.clone.1.clone | convolution fusion | flops 1827405824 | bytes 2383872 | tf_op jit(solution)/shard_map/while/body/eval_jaxpr/dot_general | solution.py:45
  57.4 2.3 %fusion.186 = f32[2304]{0:T(1024)S(1)} fusion(f32[256]{0:T(256)S(1)} %bitcast.285, f32[256]{0:T(256)S(1)} %bitcast.277, f32[2304]{0:T(1024)S(1)} %get-tuple-element.382, f32[256]{0:T(256)S(1)} %bitcast.279, f32[256]{0:T(256)S(1)} %bitcast.281, f32[2304]{0:T(1024)S(1)} %get-tuple-element.385, f32[256]{0:T(256)S(1)} %bitcast.283, f32[256]{0:T(256)S(1)} %bitcast.275), kind=kLoop, calls=%fused_computation.26.clone.1.clone | loop fusion | flops 8255232 | bytes 33792 | tf_op jit(solution)/shard_map/while/body/eval_jaxpr/reduce_sum | solution.py:48
  60.4 57.0 %while.27 = (s32[]{:T(128)}, f32[3,9,256]{2,0,1:T(4,128)S(1)}, f32[3,9,256]{2,1,0:T(8,128)S(1)}, f32[3,4,2304]{2,1,0:T(4,128)S(1)}, f32[]{:T(128)}, /*index=5*/f32[]{:T(128)}) while((s32[]{:T(128)}, f32[3,9,256]{2,0,1:T(4,128)S(1)}, f32[3,9,256]{2,1,0:T(8,128)S(1)}, f32[3,4,2304]{2,1,0:T(4,128)S(1)}, ...), condition=%wide.region_6.7_spmd.clone.clone.clone, body=%wide.region_5.6_spmd.clone.clone.sunk.clone | while | flops 3743404544 | bytes 35934480 | solution.py:177
  61.8 4.9 %fusion.201 = f32[256,2304]{0,1:T(8,128)} fusion(f32[256]{0:T(256)S(1)} %bitcast.265, f32[256]{0:T(256)S(1)} %bitcast.256, f32[2304]{0:T(1024)S(1)} %get-tuple-element.410, f32[256]{0:T(256)S(1)} %bitcast.271, f32[256]{0:T(256)S(1)} %bitcast.259, f32[2304]{0:T(1024)S(1)} %get-tuple-element.409, f32[256]{0:T(256)S(1)} %bitcast.268, ...), kind=kOutput, calls=%fused_computation.66.clone.1.clone | convolution fusion | flops 1819738112 | bytes 2383872 | tf_op jit(solution)/shard_map/while/body/eval_jaxpr/dot_general | solution.py:102
  66.8 2.1 %fusion.200 = f32[256,2304]{0,1:T(8,128)S(1)} fusion(f32[3,4,2304]{2,1,0:T(4,128)S(1)} %get-tuple-element.469, s32[]{:T(128)} %get-tuple-element.460, f32[3,9,256]{2,1,0:T(8,128)S(1)} %get-tuple-element.468, s32[]{:T(128)S(6)} %add.601), kind=kOutput, calls=%fused_computation.88.clone.1.clone | convolution fusion | flops 21233664 | bytes 2401284 | tf_op jit(solution)/shard_map/while/body/eval_jaxpr/dot_general | solution.py:106
  68.9 4.4 %fusion.202 = f32[256,2304]{0,1:T(8,128)S(1)} fusion(f32[256,2304]{0,1:T(8,128)S(1)} %fusion.200, f32[256,2304]{0,1:T(8,128)S(1)} %copy-done.1, f32[2304]{0:T(1024)S(1)} %dynamic-slice_reduce_fusion.3, f32[256]{0:T(256)S(1)} %bitcast.266, f32[256]{0:T(256)S(1)} %bitcast.257, f32[2304]{0:T(1024)S(1)} %get-tuple-element.410, ...), kind=kOutput, calls=%fused_computation.70.clone.1.clone | convolution fusion | flops 1830944768 | bytes 7111680 | tf_op jit(solution)/shard_map/while/body/eval_jaxpr/dot_general | solution.py:113
  77.0 2.2 %fusion.205 = f32[3,256]{1,0:T(4,128)S(1)} fusion(f32[256,2304]{0,1:T(8,128)S(1)} %copy-done.2, f32[256]{0:T(256)S(1)} %bitcast.267, f32[256]{0:T(256)S(1)} %bitcast.258, f32[2304]{0:T(1024)S(1)} %get-tuple-element.410, f32[256]{0:T(256)S(1)} %bitcast.273, f32[256]{0:T(256)S(1)} %bitcast.261, f32[2304]{0:T(1024)S(1)} %get-tuple-element.409, ...), kind=kOutput, calls=%fused_computation.80.clone.1.clone | convolution fusion | flops 28901376 | bytes 2429956 | tf_op jit(solution)/shard_map/while/body/eval_jaxpr/dot_general | solution.py:63
  80.7 4.9 %fusion.201 = f32[256,2304]{0,1:T(8,128)} fusion(f32[256]{0:T(256)S(1)} %bitcast.265, f32[256]{0:T(256)S(1)} %bitcast.256, f32[2304]{0:T(1024)S(1)} %get-tuple-element.410, f32[256]{0:T(256)S(1)} %bitcast.271, f32[256]{0:T(256)S(1)} %bitcast.259, f32[2304]{0:T(1024)S(1)} %get-tuple-element.409, f32[256]{0:T(256)S(1)} %bitcast.268, ...), kind=kOutput, calls=%fused_computation.66.clone.1.clone | convolution fusion | flops 1819738112 | bytes 2383872 | tf_op jit(solution)/shard_map/while/body/eval_jaxpr/dot_general | solution.py:102
  87.8 4.4 %fusion.202 = f32[256,2304]{0,1:T(8,128)S(1)} fusion(f32[256,2304]{0,1:T(8,128)S(1)} %fusion.200, f32[256,2304]{0,1:T(8,128)S(1)} %copy-done.1, f32[2304]{0:T(1024)S(1)} %dynamic-slice_reduce_fusion.3, f32[256]{0:T(256)S(1)} %bitcast.266, f32[256]{0:T(256)S(1)} %bitcast.257, f32[2304]{0:T(1024)S(1)} %get-tuple-element.410, ...), kind=kOutput, calls=%fused_computation.70.clone.1.clone | convolution fusion | flops 1830944768 | bytes 7111680 | tf_op jit(solution)/shard_map/while/body/eval_jaxpr/dot_general | solution.py:113
  95.9 2.2 %fusion.205 = f32[3,256]{1,0:T(4,128)S(1)} fusion(f32[256,2304]{0,1:T(8,128)S(1)} %copy-done.2, f32[256]{0:T(256)S(1)} %bitcast.267, f32[256]{0:T(256)S(1)} %bitcast.258, f32[2304]{0:T(1024)S(1)} %get-tuple-element.410, f32[256]{0:T(256)S(1)} %bitcast.273, f32[256]{0:T(256)S(1)} %bitcast.261, f32[2304]{0:T(1024)S(1)} %get-tuple-element.409, ...), kind=kOutput, calls=%fused_computation.80.clone.1.clone | convolution fusion | flops 28901376 | bytes 2429956 | tf_op jit(solution)/shard_map/while/body/eval_jaxpr/dot_general | solution.py:63
  99.6 4.9 %fusion.201 = f32[256,2304]{0,1:T(8,128)} fusion(f32[256]{0:T(256)S(1)} %bitcast.265, f32[256]{0:T(256)S(1)} %bitcast.256, f32[2304]{0:T(1024)S(1)} %get-tuple-element.410, f32[256]{0:T(256)S(1)} %bitcast.271, f32[256]{0:T(256)S(1)} %bitcast.259, f32[2304]{0:T(1024)S(1)} %get-tuple-element.409, f32[256]{0:T(256)S(1)} %bitcast.268, ...), kind=kOutput, calls=%fused_computation.66.clone.1.clone | convolution fusion | flops 1819738112 | bytes 2383872 | tf_op jit(solution)/shard_map/while/body/eval_jaxpr/dot_general | solution.py:102
  104.5 2.1 %fusion.200 = f32[256,2304]{0,1:T(8,128)S(1)} fusion(f32[3,4,2304]{2,1,0:T(4,128)S(1)} %get-tuple-element.469, s32[]{:T(128)} %get-tuple-element.460, f32[3,9,256]{2,1,0:T(8,128)S(1)} %get-tuple-element.468, s32[]{:T(128)S(6)} %add.601), kind=kOutput, calls=%fused_computation.88.clone.1.clone | convolution fusion | flops 21233664 | bytes 2401284 | tf_op jit(solution)/shard_map/while/body/eval_jaxpr/dot_general | solution.py:106
  106.7 4.4 %fusion.202 = f32[256,2304]{0,1:T(8,128)S(1)} fusion(f32[256,2304]{0,1:T(8,128)S(1)} %fusion.200, f32[256,2304]{0,1:T(8,128)S(1)} %copy-done.1, f32[2304]{0:T(1024)S(1)} %dynamic-slice_reduce_fusion.3, f32[256]{0:T(256)S(1)} %bitcast.266, f32[256]{0:T(256)S(1)} %bitcast.257, f32[2304]{0:T(1024)S(1)} %get-tuple-element.410, ...), kind=kOutput, calls=%fused_computation.70.clone.1.clone | convolution fusion | flops 1830944768 | bytes 7111680 | tf_op jit(solution)/shard_map/while/body/eval_jaxpr/dot_general | solution.py:113
  114.7 2.2 %fusion.205 = f32[3,256]{1,0:T(4,128)S(1)} fusion(f32[256,2304]{0,1:T(8,128)S(1)} %copy-done.2, f32[256]{0:T(256)S(1)} %bitcast.267, f32[256]{0:T(256)S(1)} %bitcast.258, f32[2304]{0:T(1024)S(1)} %get-tuple-element.410, f32[256]{0:T(256)S(1)} %bitcast.273, f32[256]{0:T(256)S(1)} %bitcast.261, f32[2304]{0:T(1024)S(1)} %get-tuple-element.409, ...), kind=kOutput, calls=%fused_computation.80.clone.1.clone | convolution fusion | flops 28901376 | bytes 2429956 | tf_op jit(solution)/shard_map/while/body/eval_jaxpr/dot_general | solution.py:63
  120.6 2.6 %collective-permute-done.4 = f32[16,9,256]{2,0,1:T(8,128)S(1)} collective-permute-done((f32[16,9,256]{2,0,1:T(8,128)S(1)}, f32[16,9,256]{2,0,1:T(8,128)S(1)}, u32[]{:S(2)}, u32[]{:S(2)}) %collective-permute-start.4) | collective-permute-done | bytes 147488 | tf_op jit(solution)/shard_map/ppermute | solution.py:14
  124.1 2.9 %collective-permute-done.6 = f32[16,9,256]{2,0,1:T(8,128)S(1)} collective-permute-done((f32[16,9,256]{2,0,1:T(8,128)S(1)}, f32[16,9,256]{2,0,1:T(8,128)S(1)}, u32[]{:S(2)}, u32[]{:S(2)}) %collective-permute-start.6) | collective-permute-done | bytes 147488 | tf_op jit(solution)/shard_map/ppermute | solution.py:14
  127.0 2.2 %collective-permute-done.7 = f32[16,9,256]{2,0,1:T(8,128)S(1)} collective-permute-done((f32[16,9,256]{2,0,1:T(8,128)S(1)}, f32[16,9,256]{2,0,1:T(8,128)S(1)}, u32[]{:S(2)}, u32[]{:S(2)}) %collective-permute-start.7) | collective-permute-done | bytes 147488 | tf_op jit(solution)/shard_map/ppermute | solution.py:14
  130.5 44.9 %all-reduce.2.cloned.1.call-done = f32[16,9,256]{2,0,1:T(8,128)} async-done(((f32[16,9,256]{2,0,1:T(8,128)}), f32[16,9,256]{2,0,1:T(8,128)}) %all-reduce.2.cloned.1.call-update) | async-done | bytes 147472 | tf_op jit(solution)/shard_map/psum | solution.py:186
  (121 shorter events, 51.4 us)
Async XLA Ops:
  7.2 168.3 %all-reduce.2.cloned.1.call-start = ((), (), s32[]{:S(2)}) async-start(), calls=%async_computation | async-start | bytes 294912 | tf_op jit(solution)/shard_map/psum | solution.py:186
  8.2 13.0 %collective-permute-start = (f32[16,9,256]{2,1,0:T(8,128)S(1)}, f32[16,9,256]{2,1,0:T(8,128)S(1)}, u32[]{:S(2)}, u32[]{:S(2)}) collective-permute-start(f32[16,9,256]{2,1,0:T(8,128)S(1)} %copy.22), channel_id=1, source_target_pairs={{248,0},{252,4},{0,8},{4,12},{8,16},{12,20},{16,24},{20,28},{24,32... | collective-permute-start | bytes 442376 | tf_op jit(solution)/shard_map/ppermute | solution.py:14
  10.2 12.9 %collective-permute-start.1 = (f32[16,9,256]{2,1,0:T(8,128)S(1)}, f32[16,9,256]{2,1,0:T(8,128)S(1)}, u32[]{:S(2)}, u32[]{:S(2)}) collective-permute-start(f32[16,9,256]{2,1,0:T(8,128)S(1)} %copy.22), channel_id=1, source_target_pairs={{252,0},{0,4},{4,8},{8,12},{12,16},{16,20},{20,24},{24,28},{28,32}... | collective-permute-start | bytes 442376 | tf_op jit(solution)/shard_map/ppermute | solution.py:14
  10.2 15.4 %collective-permute-start.2 = (f32[16,9,256]{2,1,0:T(8,128)S(1)}, f32[16,9,256]{2,1,0:T(8,128)S(1)}, u32[]{:S(2)}, u32[]{:S(2)}) collective-permute-start(f32[16,9,256]{2,1,0:T(8,128)S(1)} %copy.22), channel_id=1, source_target_pairs={{4,0},{8,4},{12,8},{16,12},{20,16},{24,20},{28,24},{32,28},{36,32}... | collective-permute-start | bytes 442376 | tf_op jit(solution)/shard_map/ppermute | solution.py:14
  14.1 12.2 %collective-permute-start.3 = (f32[16,9,256]{2,1,0:T(8,128)S(1)}, f32[16,9,256]{2,1,0:T(8,128)S(1)}, u32[]{:S(2)}, u32[]{:S(2)}) collective-permute-start(f32[16,9,256]{2,1,0:T(8,128)S(1)} %copy.22), channel_id=1, source_target_pairs={{8,0},{12,4},{16,8},{20,12},{24,16},{28,20},{32,24},{36,28},{40,32... | collective-permute-start | bytes 442376 | tf_op jit(solution)/shard_map/ppermute | solution.py:14
  29.0 31.1 %copy-start = (f32[1,1,3,2304]{3,1,2,0:T(1,128)S(1)}, f32[1,1,3,2304]{3,1,2,0:T(1,128)}, u32[]{:S(2)}) copy-start(f32[1,1,3,2304]{3,1,2,0:T(1,128)} %param.15) | copy-start | bytes 82948
  66.8 2.2 %copy-start.1 = (f32[256,2304]{0,1:T(8,128)S(1)}, f32[256,2304]{0,1:T(8,128)}, u32[]{:S(2)}) copy-start(f32[256,2304]{0,1:T(8,128)} %fusion.201) | copy-start | bytes 7077892 | tf_op jit(solution)/shard_map/while
  75.3 1.7 copy-start.2
  85.6 2.2 %copy-start.1 = (f32[256,2304]{0,1:T(8,128)S(1)}, f32[256,2304]{0,1:T(8,128)}, u32[]{:S(2)}) copy-start(f32[256,2304]{0,1:T(8,128)} %fusion.201) | copy-start | bytes 7077892 | tf_op jit(solution)/shard_map/while
  94.2 1.7 copy-start.2
  104.5 2.2 %copy-start.1 = (f32[256,2304]{0,1:T(8,128)S(1)}, f32[256,2304]{0,1:T(8,128)}, u32[]{:S(2)}) copy-start(f32[256,2304]{0,1:T(8,128)} %fusion.201) | copy-start | bytes 7077892 | tf_op jit(solution)/shard_map/while
  113.1 1.7 copy-start.2
  118.0 5.2 %collective-permute-start.4 = (f32[16,9,256]{2,0,1:T(8,128)S(1)}, f32[16,9,256]{2,0,1:T(8,128)S(1)}, u32[]{:S(2)}, u32[]{:S(2)}) collective-permute-start(f32[16,9,256]{2,0,1:T(8,128)S(1)} %get-tuple-element.244), channel_id=1, source_target_pairs={{8,0},{12,4},{16,8},{20,12},{24,16},{28,20},{32,24},{36,28},{40,32... | collective-permute-start | bytes 442376 | tf_op jit(solution)/shard_map/ppermute | solution.py:14
  119.8 4.2 %collective-permute-start.5 = (f32[16,9,256]{2,0,1:T(8,128)S(1)}, f32[16,9,256]{2,0,1:T(8,128)S(1)}, u32[]{:S(2)}, u32[]{:S(2)}) collective-permute-start(f32[16,9,256]{2,0,1:T(8,128)S(1)} %get-tuple-element.247), channel_id=1, source_target_pairs={{4,0},{8,4},{12,8},{16,12},{20,16},{24,20},{28,24},{32,28},{36,32}... | collective-permute-start | bytes 442376 | tf_op jit(solution)/shard_map/ppermute | solution.py:14
  119.8 7.2 %collective-permute-start.6 = (f32[16,9,256]{2,0,1:T(8,128)S(1)}, f32[16,9,256]{2,0,1:T(8,128)S(1)}, u32[]{:S(2)}, u32[]{:S(2)}) collective-permute-start(f32[16,9,256]{2,0,1:T(8,128)S(1)} %get-tuple-element.246), channel_id=1, source_target_pairs={{252,0},{0,4},{4,8},{8,12},{12,16},{16,20},{20,24},{24,28},{28,32}... | collective-permute-start | bytes 442376 | tf_op jit(solution)/shard_map/ppermute | solution.py:14
  120.3 8.8 %collective-permute-start.7 = (f32[16,9,256]{2,0,1:T(8,128)S(1)}, f32[16,9,256]{2,0,1:T(8,128)S(1)}, u32[]{:S(2)}, u32[]{:S(2)}) collective-permute-start(f32[16,9,256]{2,0,1:T(8,128)S(1)} %get-tuple-element.245), channel_id=1, source_target_pairs={{248,0},{252,4},{0,8},{4,12},{8,16},{12,20},{16,24},{20,28},{24,32... | collective-permute-start | bytes 442376 | tf_op jit(solution)/shard_map/ppermute | solution.py:14
Sparse Core Ops, SparseCore 0:
  130.0 45.3 all-reduce.1
where the time goes:
time: 184 us
  matrix products  64.5 us (35%)
  waiting for transfers between devices  55.8 us (30%)
  other arithmetic  23.4 us (13%)
  between operations  15.5 us (8%)
  local copies, waits for them, and re-layouts  13.4 us (7%)
  starting transfers between devices  10.3 us (6%)
    psum x1, waiting for transfers between devices, shards(): gauss_grad = lax.psum(block_grads, 'view')  44.9 us
    dot_general x3, matrix products, backward_task(): jnp.dot(lower_tri, log_trans, precision=precise, preferred_element_type=j...  14.8 us
    dot_general x3, matrix products, forward_task(): jnp.dot(lower_tri, log_trans, precision=precise, preferred_element_type=j...  13.9 us
    dot_general x3, matrix products, backward_task(): jnp.dot(upper_tri, weights * shaded, precision=precise, preferred_element...  13.2 us
    ppermute x8, waiting for transfers between devices, shifted(): return lax.ppermute(block, axis, route)  10.9 us
    ppermute x8, starting transfers between devices, shifted(): return lax.ppermute(block, axis, route)  10.3 us
    sub x6, other arithmetic, pixel_frame(): pix_y = (pixel_ids // TILE).astype(jnp.float32) - centre - shift[1]  7.23 us
    reduce_sum x3, other arithmetic, forward_task(): totals = jnp.sum(log_trans, axis=0)  6.89 us
  transfers between devices with their start and end apart: 9, of which 7 were waited for; matrix products, arithmetic and copies ran while one was open for 4% of the time, Pallas kernels for 0%

commit v1 on v0

--- a/solution.py
+++ b/solution.py
@@ -183,7 +183,7 @@
     for shift_by in range(-REACH, REACH + 1):
         if shift_by != 0:
             block_grads = block_grads + shifted(spread[shift_by + REACH], "cell", shift_by)
-    gauss_grad = lax.psum(block_grads, "view")
+    gauss_grad = jnp.sum(lax.all_gather(block_grads, "view"), axis=0)
     return (rendered[None, None], gauss_grad)
 
 

time: 184 us -> 143 us (0.78)
  the two profiles are of different devices: /device:TPU:8 before, /device:TPU:2 now
where the time goes in v1:
time: 143 us
  matrix products  64.5 us (45%)
  other arithmetic  24.4 us (17%)
  blocking collectives  13.9 us (10%)
  starting transfers between devices  13.5 us (9%)
  local copies, waits for them, and re-layouts  11.8 us (8%)
  waiting for transfers between devices  11.8 us (8%)
  between operations  2.08 us (1%)
    dot_general x3, matrix products, backward_task(): jnp.dot(lower_tri, log_trans, precision=precise, preferred_element_type=j...  14.8 us
    dot_general x3, matrix products, forward_task(): jnp.dot(lower_tri, log_trans, precision=precise, preferred_element_type=j...  13.9 us
    all_gather x1, blocking collectives, shards(): gauss_grad = jnp.sum(lax.all_gather(block_grads, 'view'), axis=0)  13.9 us
    ppermute x8, starting transfers between devices, shifted(): return lax.ppermute(block, axis, route)  13.5 us
    dot_general x3, matrix products, backward_task(): jnp.dot(upper_tri, weights * shaded, precision=precise, preferred_element...  13.2 us
    ppermute x8, waiting for transfers between devices, shifted(): return lax.ppermute(block, axis, route)  11.8 us
    sub x6, other arithmetic, pixel_frame(): pix_y = (pixel_ids // TILE).astype(jnp.float32) - centre - shift[1]  7.6 us
    reduce_sum x3, other arithmetic, forward_task(): totals = jnp.sum(log_trans, axis=0)  6.88 us
  transfers between devices with their start and end apart: 8, of which 6 were waited for; matrix products, arithmetic and copies ran while one was open for 5% of the time, Pallas kernels for 0%

profile of v1, /device:TPU:2, one launch (start us, length us, event | category | flops | bytes accessed | tf_op | source)
XLA Modules:
  0.0 142.8 jit_solution(11425719154649782178)
XLA Ops:
  3.6 6.0 %collective-permute-start.2 = (f32[16,9,256]{2,1,0:T(8,128)S(1)}, f32[16,9,256]{2,1,0:T(8,128)S(1)}, u32[]{:S(2)}, u32[]{:S(2)}) collective-permute-start(f32[16,9,256]{2,1,0:T(8,128)S(1)} %copy.22), channel_id=1, source_target_pairs={{4,0},{8,4},{12,8},{16,12},{20,16},{24,20},{28,24},{32,28},{36,32}... | collective-permute-start | bytes 442376 | tf_op jit(solution)/shard_map/ppermute | solution.py:14
  9.6 2.2 %collective-permute-start.3 = (f32[16,9,256]{2,1,0:T(8,128)S(1)}, f32[16,9,256]{2,1,0:T(8,128)S(1)}, u32[]{:S(2)}, u32[]{:S(2)}) collective-permute-start(f32[16,9,256]{2,1,0:T(8,128)S(1)} %copy.22), channel_id=1, source_target_pairs={{8,0},{12,4},{16,8},{20,12},{24,16},{28,20},{32,24},{36,28},{40,32... | collective-permute-start | bytes 442376 | tf_op jit(solution)/shard_map/ppermute | solution.py:14
  25.0 31.0 %while.26 = (s32[]{:T(128)}, f32[3,4,2304]{2,1,0:T(4,128)S(1)}, f32[3,9,256]{2,1,0:T(8,128)S(1)}, f32[]{:T(128)}, f32[]{:T(128)}) while((s32[]{:T(128)}, f32[3,4,2304]{2,1,0:T(4,128)S(1)}, f32[3,9,256]{2,1,0:T(8,128)S(1)}, f32[]{:T(128)}, f32[]{:T(128)}) %tuple.102), condition=%wide.region_2.3_spmd.clone.clone, body=%wide.region_0.2_spmd.clone.sunk.clone | while | flops 1856945664 | bytes 4940977 | solution.py:173
  26.3 4.6 %fusion.187 = f32[256,2304]{0,1:T(8,128)S(1)} fusion(f32[256]{0:T(256)S(1)} %bitcast.286, f32[256]{0:T(256)S(1)} %bitcast.278, f32[2304]{0:T(1024)S(1)} %get-tuple-element.382, f32[256]{0:T(256)S(1)} %bitcast.280, f32[256]{0:T(256)S(1)} %bitcast.282, f32[2304]{0:T(1024)S(1)} %get-tuple-element.385, f32[256]{0:T(256)S(1)} %bitcast.284, ...), kind=kOutput, calls=%fused_computation.19.clone.1.clone | convolution fusion | flops 1827405824 | bytes 2383872 | tf_op jit(solution)/shard_map/while/body/eval_jaxpr/dot_general | solution.py:45
  32.9 2.3 %fusion.186 = f32[2304]{0:T(1024)S(1)} fusion(f32[256]{0:T(256)S(1)} %bitcast.287, f32[256]{0:T(256)S(1)} %bitcast.279, f32[2304]{0:T(1024)S(1)} %get-tuple-element.382, f32[256]{0:T(256)S(1)} %bitcast.281, f32[256]{0:T(256)S(1)} %bitcast.283, f32[2304]{0:T(1024)S(1)} %get-tuple-element.385, f32[256]{0:T(256)S(1)} %bitcast.285, f32[256]{0:T(256)S(1)} %bitcast.277), kind=kLoop, calls=%fused_computation.26.clone.1.clone | loop fusion | flops 8255232 | bytes 33792 | tf_op jit(solution)/shard_map/while/body/eval_jaxpr/reduce_sum | solution.py:48
  36.6 4.6 %fusion.187 = f32[256,2304]{0,1:T(8,128)S(1)} fusion(f32[256]{0:T(256)S(1)} %bitcast.286, f32[256]{0:T(256)S(1)} %bitcast.278, f32[2304]{0:T(1024)S(1)} %get-tuple-element.382, f32[256]{0:T(256)S(1)} %bitcast.280, f32[256]{0:T(256)S(1)} %bitcast.282, f32[2304]{0:T(1024)S(1)} %get-tuple-element.385, f32[256]{0:T(256)S(1)} %bitcast.284, ...), kind=kOutput, calls=%fused_computation.19.clone.1.clone | convolution fusion | flops 1827405824 | bytes 2383872 | tf_op jit(solution)/shard_map/while/body/eval_jaxpr/dot_general | solution.py:45
  43.3 2.3 %fusion.186 = f32[2304]{0:T(1024)S(1)} fusion(f32[256]{0:T(256)S(1)} %bitcast.287, f32[256]{0:T(256)S(1)} %bitcast.279, f32[2304]{0:T(1024)S(1)} %get-tuple-element.382, f32[256]{0:T(256)S(1)} %bitcast.281, f32[256]{0:T(256)S(1)} %bitcast.283, f32[2304]{0:T(1024)S(1)} %get-tuple-element.385, f32[256]{0:T(256)S(1)} %bitcast.285, f32[256]{0:T(256)S(1)} %bitcast.277), kind=kLoop, calls=%fused_computation.26.clone.1.clone | loop fusion | flops 8255232 | bytes 33792 | tf_op jit(solution)/shard_map/while/body/eval_jaxpr/reduce_sum | solution.py:48
  46.9 4.6 %fusion.187 = f32[256,2304]{0,1:T(8,128)S(1)} fusion(f32[256]{0:T(256)S(1)} %bitcast.286, f32[256]{0:T(256)S(1)} %bitcast.278, f32[2304]{0:T(1024)S(1)} %get-tuple-element.382, f32[256]{0:T(256)S(1)} %bitcast.280, f32[256]{0:T(256)S(1)} %bitcast.282, f32[2304]{0:T(1024)S(1)} %get-tuple-element.385, f32[256]{0:T(256)S(1)} %bitcast.284, ...), kind=kOutput, calls=%fused_computation.19.clone.1.clone | convolution fusion | flops 1827405824 | bytes 2383872 | tf_op jit(solution)/shard_map/while/body/eval_jaxpr/dot_general | solution.py:45
  53.6 2.3 %fusion.186 = f32[2304]{0:T(1024)S(1)} fusion(f32[256]{0:T(256)S(1)} %bitcast.287, f32[256]{0:T(256)S(1)} %bitcast.279, f32[2304]{0:T(1024)S(1)} %get-tuple-element.382, f32[256]{0:T(256)S(1)} %bitcast.281, f32[256]{0:T(256)S(1)} %bitcast.283, f32[2304]{0:T(1024)S(1)} %get-tuple-element.385, f32[256]{0:T(256)S(1)} %bitcast.285, f32[256]{0:T(256)S(1)} %bitcast.277), kind=kLoop, calls=%fused_computation.26.clone.1.clone | loop fusion | flops 8255232 | bytes 33792 | tf_op jit(solution)/shard_map/while/body/eval_jaxpr/reduce_sum | solution.py:48
  56.6 57.7 %while.27 = (s32[]{:T(128)}, f32[3,9,256]{2,0,1:T(4,128)S(1)}, f32[3,9,256]{2,1,0:T(8,128)S(1)}, f32[3,4,2304]{2,1,0:T(4,128)S(1)}, f32[]{:T(128)}, /*index=5*/f32[]{:T(128)}) while((s32[]{:T(128)}, f32[3,9,256]{2,0,1:T(4,128)S(1)}, f32[3,9,256]{2,1,0:T(8,128)S(1)}, f32[3,4,2304]{2,1,0:T(4,128)S(1)}, ...), condition=%wide.region_6.7_spmd.clone.clone.clone, body=%wide.region_5.6_spmd.clone.clone.sunk.clone | while | flops 3743404544 | bytes 35934480 | solution.py:177
  58.1 4.9 %fusion.201 = f32[256,2304]{0,1:T(8,128)} fusion(f32[256]{0:T(256)S(1)} %bitcast.267, f32[256]{0:T(256)S(1)} %bitcast.258, f32[2304]{0:T(1024)S(1)} %get-tuple-element.410, f32[256]{0:T(256)S(1)} %bitcast.273, f32[256]{0:T(256)S(1)} %bitcast.261, f32[2304]{0:T(1024)S(1)} %get-tuple-element.409, f32[256]{0:T(256)S(1)} %bitcast.270, ...), kind=kOutput, calls=%fused_computation.66.clone.1.clone | convolution fusion | flops 1819738112 | bytes 2383872 | tf_op jit(solution)/shard_map/while/body/eval_jaxpr/dot_general | solution.py:102
  63.0 2.1 %fusion.200 = f32[256,2304]{0,1:T(8,128)S(1)} fusion(f32[3,4,2304]{2,1,0:T(4,128)S(1)} %get-tuple-element.469, s32[]{:T(128)} %get-tuple-element.460, f32[3,9,256]{2,1,0:T(8,128)S(1)} %get-tuple-element.468, s32[]{:T(128)S(6)} %add.599), kind=kOutput, calls=%fused_computation.88.clone.1.clone | convolution fusion | flops 21233664 | bytes 2401284 | tf_op jit(solution)/shard_map/while/body/eval_jaxpr/dot_general | solution.py:106
  65.2 4.4 %fusion.202 = f32[256,2304]{0,1:T(8,128)S(1)} fusion(f32[256,2304]{0,1:T(8,128)S(1)} %fusion.200, f32[256,2304]{0,1:T(8,128)S(1)} %copy-done.1, f32[2304]{0:T(1024)S(1)} %dynamic-slice_reduce_fusion.3, f32[256]{0:T(256)S(1)} %bitcast.268, f32[256]{0:T(256)S(1)} %bitcast.259, f32[2304]{0:T(1024)S(1)} %get-tuple-element.410, ...), kind=kOutput, calls=%fused_computation.70.clone.1.clone | convolution fusion | flops 1830944768 | bytes 7111680 | tf_op jit(solution)/shard_map/while/body/eval_jaxpr/dot_general | solution.py:113
  73.4 2.2 %fusion.205 = f32[3,256]{1,0:T(4,128)S(1)} fusion(f32[256,2304]{0,1:T(8,128)S(1)} %copy-done.2, f32[256]{0:T(256)S(1)} %bitcast.269, f32[256]{0:T(256)S(1)} %bitcast.260, f32[2304]{0:T(1024)S(1)} %get-tuple-element.410, f32[256]{0:T(256)S(1)} %bitcast.275, f32[256]{0:T(256)S(1)} %bitcast.263, f32[2304]{0:T(1024)S(1)} %get-tuple-element.409, ...), kind=kOutput, calls=%fused_computation.80.clone.1.clone | convolution fusion | flops 28901376 | bytes 2429956 | tf_op jit(solution)/shard_map/while/body/eval_jaxpr/dot_general | solution.py:63
  77.2 4.9 %fusion.201 = f32[256,2304]{0,1:T(8,128)} fusion(f32[256]{0:T(256)S(1)} %bitcast.267, f32[256]{0:T(256)S(1)} %bitcast.258, f32[2304]{0:T(1024)S(1)} %get-tuple-element.410, f32[256]{0:T(256)S(1)} %bitcast.273, f32[256]{0:T(256)S(1)} %bitcast.261, f32[2304]{0:T(1024)S(1)} %get-tuple-element.409, f32[256]{0:T(256)S(1)} %bitcast.270, ...), kind=kOutput, calls=%fused_computation.66.clone.1.clone | convolution fusion | flops 1819738112 | bytes 2383872 | tf_op jit(solution)/shard_map/while/body/eval_jaxpr/dot_general | solution.py:102
  84.3 4.4 %fusion.202 = f32[256,2304]{0,1:T(8,128)S(1)} fusion(f32[256,2304]{0,1:T(8,128)S(1)} %fusion.200, f32[256,2304]{0,1:T(8,128)S(1)} %copy-done.1, f32[2304]{0:T(1024)S(1)} %dynamic-slice_reduce_fusion.3, f32[256]{0:T(256)S(1)} %bitcast.268, f32[256]{0:T(256)S(1)} %bitcast.259, f32[2304]{0:T(1024)S(1)} %get-tuple-element.410, ...), kind=kOutput, calls=%fused_computation.70.clone.1.clone | convolution fusion | flops 1830944768 | bytes 7111680 | tf_op jit(solution)/shard_map/while/body/eval_jaxpr/dot_general | solution.py:113
  92.5 2.2 %fusion.205 = f32[3,256]{1,0:T(4,128)S(1)} fusion(f32[256,2304]{0,1:T(8,128)S(1)} %copy-done.2, f32[256]{0:T(256)S(1)} %bitcast.269, f32[256]{0:T(256)S(1)} %bitcast.260, f32[2304]{0:T(1024)S(1)} %get-tuple-element.410, f32[256]{0:T(256)S(1)} %bitcast.275, f32[256]{0:T(256)S(1)} %bitcast.263, f32[2304]{0:T(1024)S(1)} %get-tuple-element.409, ...), kind=kOutput, calls=%fused_computation.80.clone.1.clone | convolution fusion | flops 28901376 | bytes 2429956 | tf_op jit(solution)/shard_map/while/body/eval_jaxpr/dot_general | solution.py:63
  96.3 4.9 %fusion.201 = f32[256,2304]{0,1:T(8,128)} fusion(f32[256]{0:T(256)S(1)} %bitcast.267, f32[256]{0:T(256)S(1)} %bitcast.258, f32[2304]{0:T(1024)S(1)} %get-tuple-element.410, f32[256]{0:T(256)S(1)} %bitcast.273, f32[256]{0:T(256)S(1)} %bitcast.261, f32[2304]{0:T(1024)S(1)} %get-tuple-element.409, f32[256]{0:T(256)S(1)} %bitcast.270, ...), kind=kOutput, calls=%fused_computation.66.clone.1.clone | convolution fusion | flops 1819738112 | bytes 2383872 | tf_op jit(solution)/shard_map/while/body/eval_jaxpr/dot_general | solution.py:102
  103.4 4.4 %fusion.202 = f32[256,2304]{0,1:T(8,128)S(1)} fusion(f32[256,2304]{0,1:T(8,128)S(1)} %fusion.200, f32[256,2304]{0,1:T(8,128)S(1)} %copy-done.1, f32[2304]{0:T(1024)S(1)} %dynamic-slice_reduce_fusion.3, f32[256]{0:T(256)S(1)} %bitcast.268, f32[256]{0:T(256)S(1)} %bitcast.259, f32[2304]{0:T(1024)S(1)} %get-tuple-element.410, ...), kind=kOutput, calls=%fused_computation.70.clone.1.clone | convolution fusion | flops 1830944768 | bytes 7111680 | tf_op jit(solution)/shard_map/while/body/eval_jaxpr/dot_general | solution.py:113
  111.6 2.2 %fusion.205 = f32[3,256]{1,0:T(4,128)S(1)} fusion(f32[256,2304]{0,1:T(8,128)S(1)} %copy-done.2, f32[256]{0:T(256)S(1)} %bitcast.269, f32[256]{0:T(256)S(1)} %bitcast.260, f32[2304]{0:T(1024)S(1)} %get-tuple-element.410, f32[256]{0:T(256)S(1)} %bitcast.275, f32[256]{0:T(256)S(1)} %bitcast.263, f32[2304]{0:T(1024)S(1)} %get-tuple-element.409, ...), kind=kOutput, calls=%fused_computation.80.clone.1.clone | convolution fusion | flops 28901376 | bytes 2429956 | tf_op jit(solution)/shard_map/while/body/eval_jaxpr/dot_general | solution.py:63
  114.9 2.7 %collective-permute-start.4 = (f32[16,9,256]{2,0,1:T(8,128)S(1)}, f32[16,9,256]{2,0,1:T(8,128)S(1)}, u32[]{:S(2)}, u32[]{:S(2)}) collective-permute-start(f32[16,9,256]{2,0,1:T(8,128)S(1)} %get-tuple-element.244), channel_id=1, source_target_pairs={{8,0},{12,4},{16,8},{20,12},{24,16},{28,20},{32,24},{36,28},{40,32... | collective-permute-start | bytes 442376 | tf_op jit(solution)/shard_map/ppermute | solution.py:14
  121.9 4.1 %collective-permute-done.6 = f32[16,9,256]{2,0,1:T(8,128)S(1)} collective-permute-done((f32[16,9,256]{2,0,1:T(8,128)S(1)}, f32[16,9,256]{2,0,1:T(8,128)S(1)}, u32[]{:S(2)}, u32[]{:S(2)}) %collective-permute-start.6) | collective-permute-done | bytes 147488 | tf_op jit(solution)/shard_map/ppermute | solution.py:14
  126.0 2.2 %collective-permute-done.7 = f32[16,9,256]{2,0,1:T(8,128)S(1)} collective-permute-done((f32[16,9,256]{2,0,1:T(8,128)S(1)}, f32[16,9,256]{2,0,1:T(8,128)S(1)}, u32[]{:S(2)}, u32[]{:S(2)}) %collective-permute-start.7) | collective-permute-done | bytes 147488 | tf_op jit(solution)/shard_map/ppermute | solution.py:14
  128.2 13.9 %all-gather = f32[64,9,256]{2,0,1:T(8,128)S(1)} all-gather(f32[16,9,256]{2,0,1:T(8,128)S(1)} %fusion.110), channel_id=2, replica_groups=mesh['cell'=64,'view'=4] {'view'}, dimensions={0}, use_global_device_ids=true | all-gather | bytes 737280 | tf_op jit(solution)/shard_map/all_gather | solution.py:186
  (119 shorter events, 51.2 us)
Async XLA Ops:
  1.6 15.5 %collective-permute-start = (f32[16,9,256]{2,1,0:T(8,128)S(1)}, f32[16,9,256]{2,1,0:T(8,128)S(1)}, u32[]{:S(2)}, u32[]{:S(2)}) collective-permute-start(f32[16,9,256]{2,1,0:T(8,128)S(1)} %copy.22), channel_id=1, source_target_pairs={{248,0},{252,4},{0,8},{4,12},{8,16},{12,20},{16,24},{20,28},{24,32... | collective-permute-start | bytes 442376 | tf_op jit(solution)/shard_map/ppermute | solution.py:14
  3.6 15.5 %collective-permute-start.1 = (f32[16,9,256]{2,1,0:T(8,128)S(1)}, f32[16,9,256]{2,1,0:T(8,128)S(1)}, u32[]{:S(2)}, u32[]{:S(2)}) collective-permute-start(f32[16,9,256]{2,1,0:T(8,128)S(1)} %copy.22), channel_id=1, source_target_pairs={{252,0},{0,4},{4,8},{8,12},{12,16},{16,20},{20,24},{24,28},{28,32}... | collective-permute-start | bytes 442376 | tf_op jit(solution)/shard_map/ppermute | solution.py:14
  3.6 17.9 %collective-permute-start.2 = (f32[16,9,256]{2,1,0:T(8,128)S(1)}, f32[16,9,256]{2,1,0:T(8,128)S(1)}, u32[]{:S(2)}, u32[]{:S(2)}) collective-permute-start(f32[16,9,256]{2,1,0:T(8,128)S(1)} %copy.22), channel_id=1, source_target_pairs={{4,0},{8,4},{12,8},{16,12},{20,16},{24,20},{28,24},{32,28},{36,32}... | collective-permute-start | bytes 442376 | tf_op jit(solution)/shard_map/ppermute | solution.py:14
  9.6 12.7 %collective-permute-start.3 = (f32[16,9,256]{2,1,0:T(8,128)S(1)}, f32[16,9,256]{2,1,0:T(8,128)S(1)}, u32[]{:S(2)}, u32[]{:S(2)}) collective-permute-start(f32[16,9,256]{2,1,0:T(8,128)S(1)} %copy.22), channel_id=1, source_target_pairs={{8,0},{12,4},{16,8},{20,12},{24,16},{28,20},{32,24},{36,28},{40,32... | collective-permute-start | bytes 442376 | tf_op jit(solution)/shard_map/ppermute | solution.py:14
  25.0 31.3 %copy-start = (f32[1,1,3,2304]{3,1,2,0:T(1,128)S(1)}, f32[1,1,3,2304]{3,1,2,0:T(1,128)}, u32[]{:S(2)}) copy-start(f32[1,1,3,2304]{3,1,2,0:T(1,128)} %param.15) | copy-start | bytes 82948
  63.0 2.2 %copy-start.1 = (f32[256,2304]{0,1:T(8,128)S(1)}, f32[256,2304]{0,1:T(8,128)}, u32[]{:S(2)}) copy-start(f32[256,2304]{0,1:T(8,128)} %fusion.201) | copy-start | bytes 7077892 | tf_op jit(solution)/shard_map/while
  71.8 1.7 %copy-start.2 = (f32[256,2304]{0,1:T(8,128)S(1)}, f32[256,2304]{0,1:T(8,128)}, u32[]{:S(2)}) copy-start(f32[256,2304]{0,1:T(8,128)} %fusion.201) | copy-start | bytes 7077892 | tf_op jit(solution)/shard_map/while
  82.1 2.2 %copy-start.1 = (f32[256,2304]{0,1:T(8,128)S(1)}, f32[256,2304]{0,1:T(8,128)}, u32[]{:S(2)}) copy-start(f32[256,2304]{0,1:T(8,128)} %fusion.201) | copy-start | bytes 7077892 | tf_op jit(solution)/shard_map/while
  90.9 1.7 %copy-start.2 = (f32[256,2304]{0,1:T(8,128)S(1)}, f32[256,2304]{0,1:T(8,128)}, u32[]{:S(2)}) copy-start(f32[256,2304]{0,1:T(8,128)} %fusion.201) | copy-start | bytes 7077892 | tf_op jit(solution)/shard_map/while
  101.2 2.2 %copy-start.1 = (f32[256,2304]{0,1:T(8,128)S(1)}, f32[256,2304]{0,1:T(8,128)}, u32[]{:S(2)}) copy-start(f32[256,2304]{0,1:T(8,128)} %fusion.201) | copy-start | bytes 7077892 | tf_op jit(solution)/shard_map/while
  110.0 1.7 %copy-start.2 = (f32[256,2304]{0,1:T(8,128)S(1)}, f32[256,2304]{0,1:T(8,128)}, u32[]{:S(2)}) copy-start(f32[256,2304]{0,1:T(8,128)} %fusion.201) | copy-start | bytes 7077892 | tf_op jit(solution)/shard_map/while
  114.9 5.4 %collective-permute-start.4 = (f32[16,9,256]{2,0,1:T(8,128)S(1)}, f32[16,9,256]{2,0,1:T(8,128)S(1)}, u32[]{:S(2)}, u32[]{:S(2)}) collective-permute-start(f32[16,9,256]{2,0,1:T(8,128)S(1)} %get-tuple-element.244), channel_id=1, source_target_pairs={{8,0},{12,4},{16,8},{20,12},{24,16},{28,20},{32,24},{36,28},{40,32... | collective-permute-start | bytes 442376 | tf_op jit(solution)/shard_map/ppermute | solution.py:14
  117.6 4.2 %collective-permute-start.5 = (f32[16,9,256]{2,0,1:T(8,128)S(1)}, f32[16,9,256]{2,0,1:T(8,128)S(1)}, u32[]{:S(2)}, u32[]{:S(2)}) collective-permute-start(f32[16,9,256]{2,0,1:T(8,128)S(1)} %get-tuple-element.247), channel_id=1, source_target_pairs={{4,0},{8,4},{12,8},{16,12},{20,16},{24,20},{28,24},{32,28},{36,32}... | collective-permute-start | bytes 442376 | tf_op jit(solution)/shard_map/ppermute | solution.py:14
  117.6 8.4 %collective-permute-start.6 = (f32[16,9,256]{2,0,1:T(8,128)S(1)}, f32[16,9,256]{2,0,1:T(8,128)S(1)}, u32[]{:S(2)}, u32[]{:S(2)}) collective-permute-start(f32[16,9,256]{2,0,1:T(8,128)S(1)} %get-tuple-element.246), channel_id=1, source_target_pairs={{252,0},{0,4},{4,8},{8,12},{12,16},{16,20},{20,24},{24,28},{28,32}... | collective-permute-start | bytes 442376 | tf_op jit(solution)/shard_map/ppermute | solution.py:14
  118.1 10.0 %collective-permute-start.7 = (f32[16,9,256]{2,0,1:T(8,128)S(1)}, f32[16,9,256]{2,0,1:T(8,128)S(1)}, u32[]{:S(2)}, u32[]{:S(2)}) collective-permute-start(f32[16,9,256]{2,0,1:T(8,128)S(1)} %get-tuple-element.245), channel_id=1, source_target_pairs={{248,0},{252,4},{0,8},{4,12},{8,16},{12,20},{16,24},{20,28},{24,32... | collective-permute-start | bytes 442376 | tf_op jit(solution)/shard_map/ppermute | solution.py:14
